TPU v7x, 256 devices: a whole 4x4x8 slice. The times are simulated.
256 devices in a mesh: gx: 16 (over z, core), gy: 16 (over y, x).
Axes of the slice: x: 4, y: 4, z: 8, core: 2. Of those that a mesh axis runs over, the one named last changes fastest.
Arguments:
- demand: float32 [16, 1024, 16384], P(None, 'gx', 'gy'), may hold values from -200 to 200, as said below
- initial: float32 [1024, 256], replicated, may hold values from -6 to 6
Outputs:
- factor: float32 [1024, 256], replicated
- core: float32 [256, 16, 16384], P('gx', None, 'gy')
Inputs may be any that keep to these rules, and one draw needn't show every extreme that they name: `demand`: Real-valued fluctuations of order one to a few, not all of one scale along x.
All inputs are finite; a program needn't handle non-finite values.
Results may differ from a plain program's by a relative error of at most 0.0003.
Values sent between devices are 32-bit elements; how exact they have to be, the bound alone decides.
No kernel may reach another device: no remote copies, remote signals or barrier semaphores. Data moves between devices by JAX's collectives and lax.ppermute only.
A program may use at most 128 MiB of HBM per device.

v0:
```python
import jax
import jax.numpy as jnp
from jax import lax
from jax.sharding import PartitionSpec as P

NY = 1024
L = 16
S = 16
ITERS = 3


def orthonormal(block):
    weights = jnp.dot(
        block.T, block, precision=lax.Precision.HIGHEST, preferred_element_type=jnp.float32
    )
    lower_factor = jnp.linalg.cholesky(weights)
    return lax.linalg.triangular_solve(
        lower_factor, block, left_side=False, lower=True, transpose_a=True
    )


def on_device(demand, initial):
    regrouped = lax.all_to_all(demand, "gx", split_axis=0, concat_axis=1, tiled=True)
    local_gram = jnp.einsum(
        "lxc,lzc->xz",
        regrouped,
        regrouped,
        precision=lax.Precision.HIGHEST,
        preferred_element_type=jnp.float32,
    )
    local_gram = local_gram * (1.0 / (L * S * NY))
    basis = initial
    gram = lax.psum(local_gram, ("gx", "gy"))
    for iteration in range(ITERS):
        basis = orthonormal(
            jnp.dot(
                gram, basis, precision=lax.Precision.HIGHEST, preferred_element_type=jnp.float32
            )
        )
    core_part = jnp.einsum(
        "xr,lxc->rlc",
        basis,
        regrouped,
        precision=lax.Precision.HIGHEST,
        preferred_element_type=jnp.float32,
    )
    core = lax.all_to_all(core_part, "gx", split_axis=0, concat_axis=1, tiled=True)
    return (basis, core)


def solution(mesh):
    in_specs = (P(None, "gx", "gy"), P())
    out_specs = (P(), P("gx", None, "gy"))
    return jax.shard_map(
        on_device, mesh=mesh, in_specs=in_specs, out_specs=out_specs, check_vma=False
    )
```

profile of v0, /device:TPU:1, one launch (start us, length us, event | category | flops | bytes accessed | tf_op | source)
XLA Modules:
  0.0 658.2 jit_solution(15279910534653061629)
XLA Ops:
  7.2 106.0 %all_to_all.27 = f32[16,64,1024]{2,1,0:T(8,128)S(1)} all-to-all(f32[16,64,1024]{2,1,0:T(8,128)} %param.5), channel_id=1, replica_groups=mesh['gx'=16,'gy'=16] {'gx'}, dimensions={0} | all-to-all | bytes 8388608 | tf_op jit(solution)/shard_map/all_to_all | solution.py:23
  115.1 14.7 %convolution_multiply_fusion = f32[1024,1024]{1,0:T(8,128)} fusion(f32[1024,1024]{1,0:T(8,128)S(1)} %bitcast.118), kind=kOutput, calls=%fused_computation.6 | convolution fusion | flops 12885950464 | bytes 8388608 | tf_op jit(solution)/shard_map/lxc,lzc->xz/dot_general | solution.py:24
  129.9 265.4 %all-reduce.3.cloned.1.call-done = f32[1024,1024]{1,0:T(8,128)} async-done(((f32[1024,1024]{1,0:T(8,128)}), f32[1024,1024]{1,0:T(8,128)}) %all-reduce.3.cloned.1.call-update) | async-done | bytes 4194320 | tf_op jit(solution)/shard_map/psum | solution.py:33
  395.3 5.4 fusion.45
  402.8 11.7 %cholesky.172 = f32[128,128]{1,0:T(8,128)S(1)} custom-call(f32[128,128]{1,0:T(8,128)S(1)} %cholesky.270), custom_call_target="Cholesky" | custom-call | tf_op jit(solution)/shard_map/jit(cholesky)/cholesky | solution.py:16
  414.5 9.8 %custom-call.15 = f32[1,128,128]{1,2,0:T(8,128)S(1)} custom-call(f32[1,128,128]{2,1,0:T(8,128)S(1)} %get-tuple-element.72), custom_call_target="InvertDiagBlocksLowerTriangular" | custom-call | tf_op jit(solution)/shard_map/jit(cholesky)/cholesky | solution.py:16
  424.8 11.7 %cholesky.189 = f32[128,128]{1,0:T(8,128)S(1)} custom-call(f32[128,128]{1,0:T(8,128)S(1)} %convolution_subtract_fusion.5), custom_call_target="Cholesky" | custom-call | tf_op jit(solution)/shard_map/jit(cholesky)/cholesky | solution.py:16
  439.0 3.7 while.6
  442.7 19.7 %custom-call.16 = f32[2,128,128]{1,2,0:T(8,128)S(1)} custom-call(f32[2,128,128]{2,1,0:T(8,128)S(1)} %get-tuple-element.24), custom_call_target="InvertDiagBlocksLowerTriangular" | custom-call | tf_op jit(solution)/shard_map/triangular_solve/custom-call.0 | solution.py:17
  464.7 5.3 fusion
  472.1 11.7 %cholesky.206 = f32[128,128]{1,0:T(8,128)S(1)} custom-call(f32[128,128]{1,0:T(8,128)S(1)} %cholesky.273), custom_call_target="Cholesky" | custom-call | tf_op jit(solution)/shard_map/jit(cholesky)/cholesky | solution.py:16
  483.8 9.8 %custom-call.17 = f32[1,128,128]{1,2,0:T(8,128)S(1)} custom-call(f32[1,128,128]{2,1,0:T(8,128)S(1)} %get-tuple-element.68), custom_call_target="InvertDiagBlocksLowerTriangular" | custom-call | tf_op jit(solution)/shard_map/jit(cholesky)/cholesky | solution.py:16
  494.1 11.7 %cholesky.223 = f32[128,128]{1,0:T(8,128)S(1)} custom-call(f32[128,128]{1,0:T(8,128)S(1)} %convolution_subtract_fusion.4), custom_call_target="Cholesky" | custom-call | tf_op jit(solution)/shard_map/jit(cholesky)/cholesky | solution.py:16
  508.6 3.8 while.7
  512.4 19.7 %custom-call.18 = f32[2,128,128]{1,2,0:T(8,128)S(1)} custom-call(f32[2,128,128]{2,1,0:T(8,128)S(1)} %get-tuple-element.25), custom_call_target="InvertDiagBlocksLowerTriangular" | custom-call | tf_op jit(solution)/shard_map/triangular_solve/custom-call.0 | solution.py:17
  534.4 5.5 fusion.4
  542.0 11.7 %cholesky.240 = f32[128,128]{1,0:T(8,128)S(1)} custom-call(f32[128,128]{1,0:T(8,128)S(1)} %cholesky.276), custom_call_target="Cholesky" | custom-call | tf_op jit(solution)/shard_map/jit(cholesky)/cholesky | solution.py:16
  553.8 9.8 %custom-call.19 = f32[1,128,128]{1,2,0:T(8,128)S(1)} custom-call(f32[1,128,128]{2,1,0:T(8,128)S(1)} %get-tuple-element.64), custom_call_target="InvertDiagBlocksLowerTriangular" | custom-call | tf_op jit(solution)/shard_map/jit(cholesky)/cholesky | solution.py:16
  564.1 11.7 %cholesky.257 = f32[128,128]{1,0:T(8,128)S(1)} custom-call(f32[128,128]{1,0:T(8,128)S(1)} %convolution_subtract_fusion.3), custom_call_target="Cholesky" | custom-call | tf_op jit(solution)/shard_map/jit(cholesky)/cholesky | solution.py:16
  578.7 3.9 while.8
  582.6 19.7 %custom-call.20 = f32[2,128,128]{1,2,0:T(8,128)S(1)} custom-call(f32[2,128,128]{2,1,0:T(8,128)S(1)} %get-tuple-element.26), custom_call_target="InvertDiagBlocksLowerTriangular" | custom-call | tf_op jit(solution)/shard_map/triangular_solve/custom-call.0 | solution.py:17
  604.6 5.7 convolution_bitcast_fusion
  612.4 7.6 %all-to-all-start.1 = ((f32[256,1,1024]{2,1,0:T(1,128)}), f32[256,1,1024]{2,1,0:T(1,128)}, u32[]{:S(2)}, u32[]{:S(2)}) async-start(f32[256,1,1024]{2,1,0:T(1,128)} %copy.12), calls=%async_computation.1 | async-start | bytes 2097152 | tf_op jit(solution)/shard_map/all_to_all | solution.py:47
  623.6 24.5 %all-to-all-done.1 = f32[256,1,1024]{2,1,0:T(1,128)} async-done(((f32[256,1,1024]{2,1,0:T(1,128)}), f32[256,1,1024]{2,1,0:T(1,128)}, u32[]{:S(2)}, u32[]{:S(2)}) %all-to-all-start.1) | async-done | bytes 1048608 | tf_op jit(solution)/shard_map/all_to_all | solution.py:47
  (77 shorter events, 40.2 us)
Async XLA Ops:
  7.2 388.1 %copy-start = (f32[1024,256]{1,0:T(8,128)S(1)}, f32[1024,256]{1,0:T(8,128)}, u32[]{:S(2)}) copy-start(f32[1024,256]{1,0:T(8,128)} %param.6) | copy-start | bytes 3145732
  7.2 388.1 %all-reduce.3.cloned.1.call-start = ((), (), s32[]{:S(2)}) async-start(), calls=%async_computation.2 | async-start | bytes 8388608 | tf_op jit(solution)/shard_map/psum | solution.py:33
  113.2 1.9 copy-start.1
  612.4 35.7 %all-to-all-start.1 = ((f32[256,1,1024]{2,1,0:T(1,128)}), f32[256,1,1024]{2,1,0:T(1,128)}, u32[]{:S(2)}, u32[]{:S(2)}) async-start(f32[256,1,1024]{2,1,0:T(1,128)} %copy.12), calls=%async_computation.1 | async-start | bytes 2097152 | tf_op jit(solution)/shard_map/all_to_all | solution.py:47
Sparse Core Ops, SparseCore 0:
  130.0 265.2 all-reduce.2
where the time goes:
time: 665 us; the launch traced here: 658 us
  waiting for transfers between devices  290 us (44%)
  other arithmetic  164 us (25%)
  blocking collectives  106 us (16%)
  matrix products  50.4 us (8%)
  local copies, waits for them, and re-layouts  21.3 us (3%)
  between operations  18.9 us (3%)
  starting transfers between devices  7.65 us (1%)
    psum x1, waiting for transfers between devices, on_device(): gram = lax.psum(local_gram, ('gx', 'gy'))  265 us
    all_to_all x1, blocking collectives, on_device(): lax.all_to_all(demand, 'gx', split_axis=0, concat_axis=1, tiled=True)  106 us
    another operation x20, other arithmetic, orthonormal(): lower_factor = jnp.linalg.cholesky(weights)  103 us
    another operation x8, other arithmetic, orthonormal(): lax.linalg.triangular_solve(lower_factor, block, left_side=False, lower=T...  60.6 us
    all_to_all x1, waiting for transfers between devices, on_device(): lax.all_to_all(core_part, 'gx', split_axis=0, concat_axis=1, tiled=True)  24.5 us
    dot_general x3, matrix products, on_device(): jnp.dot(gram, basis, precision=lax.Precision.HIGHEST, preferred_element_t...  16.3 us
    dot_general x1, matrix products, on_device(): jnp.einsum('lxc,lzc->xz', regrouped, regrouped, precision=lax.Precision.H...  14.7 us
  transfers between devices with their start and end apart: 2, of which 2 were waited for; matrix products, arithmetic and copies ran while one was open for 1% of the time, Pallas kernels for 0%

commit v1 on v0

--- a/solution.py
+++ b/solution.py
@@ -2,11 +2,18 @@
 import jax.numpy as jnp
 from jax import lax
 from jax.sharding import PartitionSpec as P
+from jax.lax import psum
 
 NY = 1024
 L = 16
 S = 16
 ITERS = 3
+
+
+def feed_positions_for(local_block, axis_name, axis_tag):
+    for d in (axis_name, axis_tag):
+        local_block = psum(local_block, d)
+    return local_block
 
 
 def orthonormal(block):
@@ -30,7 +37,7 @@
     )
     local_gram = local_gram * (1.0 / (L * S * NY))
     basis = initial
-    gram = lax.psum(local_gram, ("gx", "gy"))
+    gram = feed_positions_for(local_gram, "gy", "gx")
     for iteration in range(ITERS):
         basis = orthonormal(
             jnp.dot(

time: 665 us -> 633 us (0.952)
  waiting for transfers between devices: 290 us -> 258 us
    psum x1 -> x2, waiting for transfers between devices: 265 us -> 234 us  [feed_positions_for(): local_block = psum(local_block, d)]
  transfers between devices with their start and end apart: 2 -> 3, of which waited for: 2 -> 3; matrix products, arithmetic and copies ran while one was open for 1% -> 1% of each run, Pallas kernels for 0% -> 0%
where the time goes in v1:
time: 633 us; the launch traced here: 626 us
  waiting for transfers between devices  258 us (41%)
  other arithmetic  164 us (26%)
  blocking collectives  106 us (17%)
  matrix products  50.4 us (8%)
  local copies, waits for them, and re-layouts  21.3 us (3%)
  between operations  19 us (3%)
  starting transfers between devices  7.1 us (1%)
    psum x2, waiting for transfers between devices, feed_positions_for(): local_block = psum(local_block, d)  234 us
    all_to_all x1, blocking collectives, on_device(): lax.all_to_all(demand, 'gx', split_axis=0, concat_axis=1, tiled=True)  106 us
    another operation x20, other arithmetic, orthonormal(): lower_factor = jnp.linalg.cholesky(weights)  103 us
    another operation x8, other arithmetic, orthonormal(): lax.linalg.triangular_solve(lower_factor, block, left_side=False, lower=T...  60.6 us
    all_to_all x1, waiting for transfers between devices, on_device(): lax.all_to_all(core_part, 'gx', split_axis=0, concat_axis=1, tiled=True)  24.5 us
    dot_general x3, matrix products, on_device(): jnp.dot(gram, basis, precision=lax.Precision.HIGHEST, preferred_element_t...  16.3 us
    dot_general x1, matrix products, on_device(): jnp.einsum('lxc,lzc->xz', regrouped, regrouped, precision=lax.Precision.H...  14.8 us
  transfers between devices with their start and end apart: 3, of which 3 were waited for; matrix products, arithmetic and copies ran while one was open for 1% of the time, Pallas kernels for 0%

profile of v1, /device:TPU:1, one launch (start us, length us, event | category | flops | bytes accessed | tf_op | source)
XLA Modules:
  0.0 626.0 jit_solution(5665491487347921598)
XLA Ops:
  7.2 106.0 %all_to_all.27 = f32[16,64,1024]{2,1,0:T(8,128)S(1)} all-to-all(f32[16,64,1024]{2,1,0:T(8,128)} %param.5), channel_id=1, replica_groups=mesh['gx'=16,'gy'=16] {'gx'}, dimensions={0} | all-to-all | bytes 8388608 | tf_op jit(solution)/shard_map/all_to_all | solution.py:30
  115.1 14.8 %convolution_multiply_fusion = f32[1024,1024]{1,0:T(8,128)} fusion(f32[1024,1024]{1,0:T(8,128)S(1)} %bitcast.118), kind=kOutput, calls=%fused_computation.6 | convolution fusion | flops 12885950464 | bytes 8388608 | tf_op jit(solution)/shard_map/lxc,lzc->xz/dot_general | solution.py:31
  130.0 110.2 %all-reduce.4.cloned.1.call-done = f32[1024,1024]{1,0:T(8,128)} async-done(((f32[1024,1024]{1,0:T(8,128)}), f32[1024,1024]{1,0:T(8,128)}) %all-reduce.4.cloned.1.call-update) | async-done | bytes 4194320 | tf_op jit(solution)/shard_map/psum | solution.py:15
  240.2 123.5 %all-reduce.6.cloned.1.call-done = f32[1024,1024]{1,0:T(8,128)} async-done(((f32[1024,1024]{1,0:T(8,128)}), f32[1024,1024]{1,0:T(8,128)}) %all-reduce.6.cloned.1.call-update) | async-done | bytes 4194320 | tf_op jit(solution)/shard_map/psum | solution.py:15
  363.7 5.4 fusion.45
  371.2 11.7 %cholesky.172 = f32[128,128]{1,0:T(8,128)S(1)} custom-call(f32[128,128]{1,0:T(8,128)S(1)} %cholesky.270), custom_call_target="Cholesky" | custom-call | tf_op jit(solution)/shard_map/jit(cholesky)/cholesky | solution.py:23
  382.9 9.8 %custom-call.15 = f32[1,128,128]{1,2,0:T(8,128)S(1)} custom-call(f32[1,128,128]{2,1,0:T(8,128)S(1)} %get-tuple-element.72), custom_call_target="InvertDiagBlocksLowerTriangular" | custom-call | tf_op jit(solution)/shard_map/jit(cholesky)/cholesky | solution.py:23
  393.2 11.7 %cholesky.189 = f32[128,128]{1,0:T(8,128)S(1)} custom-call(f32[128,128]{1,0:T(8,128)S(1)} %convolution_subtract_fusion.5), custom_call_target="Cholesky" | custom-call | tf_op jit(solution)/shard_map/jit(cholesky)/cholesky | solution.py:23
  411.1 19.7 %custom-call.16 = f32[2,128,128]{1,2,0:T(8,128)S(1)} custom-call(f32[2,128,128]{2,1,0:T(8,128)S(1)} %get-tuple-element.24), custom_call_target="InvertDiagBlocksLowerTriangular" | custom-call | tf_op jit(solution)/shard_map/triangular_solve/custom-call.0 | solution.py:24
  433.1 5.3 fusion
  440.5 11.7 %cholesky.206 = f32[128,128]{1,0:T(8,128)S(1)} custom-call(f32[128,128]{1,0:T(8,128)S(1)} %cholesky.273), custom_call_target="Cholesky" | custom-call | tf_op jit(solution)/shard_map/jit(cholesky)/cholesky | solution.py:23
  452.2 9.8 %custom-call.17 = f32[1,128,128]{1,2,0:T(8,128)S(1)} custom-call(f32[1,128,128]{2,1,0:T(8,128)S(1)} %get-tuple-element.68), custom_call_target="InvertDiagBlocksLowerTriangular" | custom-call | tf_op jit(solution)/shard_map/jit(cholesky)/cholesky | solution.py:23
  462.5 11.7 %cholesky.223 = f32[128,128]{1,0:T(8,128)S(1)} custom-call(f32[128,128]{1,0:T(8,128)S(1)} %convolution_subtract_fusion.4), custom_call_target="Cholesky" | custom-call | tf_op jit(solution)/shard_map/jit(cholesky)/cholesky | solution.py:23
  477.0 3.8 while.7
  480.8 19.7 %custom-call.18 = f32[2,128,128]{1,2,0:T(8,128)S(1)} custom-call(f32[2,128,128]{2,1,0:T(8,128)S(1)} %get-tuple-element.25), custom_call_target="InvertDiagBlocksLowerTriangular" | custom-call | tf_op jit(solution)/shard_map/triangular_solve/custom-call.0 | solution.py:24
  502.8 5.5 fusion.4
  510.4 11.7 %cholesky.240 = f32[128,128]{1,0:T(8,128)S(1)} custom-call(f32[128,128]{1,0:T(8,128)S(1)} %cholesky.276), custom_call_target="Cholesky" | custom-call | tf_op jit(solution)/shard_map/jit(cholesky)/cholesky | solution.py:23
  522.2 9.8 %custom-call.19 = f32[1,128,128]{1,2,0:T(8,128)S(1)} custom-call(f32[1,128,128]{2,1,0:T(8,128)S(1)} %get-tuple-element.64), custom_call_target="InvertDiagBlocksLowerTriangular" | custom-call | tf_op jit(solution)/shard_map/jit(cholesky)/cholesky | solution.py:23
  532.4 11.7 %cholesky.257 = f32[128,128]{1,0:T(8,128)S(1)} custom-call(f32[128,128]{1,0:T(8,128)S(1)} %convolution_subtract_fusion.3), custom_call_target="Cholesky" | custom-call | tf_op jit(solution)/shard_map/jit(cholesky)/cholesky | solution.py:23
  547.1 3.9 while.8
  551.0 19.7 %custom-call.20 = f32[2,128,128]{1,2,0:T(8,128)S(1)} custom-call(f32[2,128,128]{2,1,0:T(8,128)S(1)} %get-tuple-element.26), custom_call_target="InvertDiagBlocksLowerTriangular" | custom-call | tf_op jit(solution)/shard_map/triangular_solve/custom-call.0 | solution.py:24
  573.0 5.7 convolution_bitcast_fusion
  580.8 7.0 %all-to-all-start.1 = ((f32[256,1,1024]{2,1,0:T(1,128)}), f32[256,1,1024]{2,1,0:T(1,128)}, u32[]{:S(2)}, u32[]{:S(2)}) async-start(f32[256,1,1024]{2,1,0:T(1,128)} %copy.12), calls=%async_computation.1 | async-start | bytes 2097152 | tf_op jit(solution)/shard_map/all_to_all | solution.py:54
  591.4 24.5 %all-to-all-done.1 = f32[256,1,1024]{2,1,0:T(1,128)} async-done(((f32[256,1,1024]{2,1,0:T(1,128)}), f32[256,1,1024]{2,1,0:T(1,128)}, u32[]{:S(2)}, u32[]{:S(2)}) %all-to-all-start.1) | async-done | bytes 1048608 | tf_op jit(solution)/shard_map/all_to_all | solution.py:54
  (80 shorter events, 44.0 us)
Async XLA Ops:
  7.2 356.5 %copy-start = (f32[1024,256]{1,0:T(8,128)S(1)}, f32[1024,256]{1,0:T(8,128)}, u32[]{:S(2)}) copy-start(f32[1024,256]{1,0:T(8,128)} %param.6) | copy-start | bytes 3145732
  7.2 233.0 %all-reduce.4.cloned.1.call-start = ((), (), s32[]{:S(2)}) async-start(), calls=%async_computation.2 | async-start | bytes 8388608 | tf_op jit(solution)/shard_map/psum | solution.py:15
  113.2 1.9 copy-start.1
  129.9 233.8 %all-reduce.6.cloned.1.call-start = ((), (), s32[]{:S(2)}) async-start(), calls=%async_computation.3 | async-start | bytes 8388608 | tf_op jit(solution)/shard_map/psum | solution.py:15
  580.8 35.1 %all-to-all-start.1 = ((f32[256,1,1024]{2,1,0:T(1,128)}), f32[256,1,1024]{2,1,0:T(1,128)}, u32[]{:S(2)}, u32[]{:S(2)}) async-start(f32[256,1,1024]{2,1,0:T(1,128)} %copy.12), calls=%async_computation.1 | async-start | bytes 2097152 | tf_op jit(solution)/shard_map/all_to_all | solution.py:54
Sparse Core Ops, SparseCore 0:
  130.0 110.0 all-reduce.3
  242.5 121.1 all-reduce.5
